TPU v7x, 512 devices: a whole 4x8x8 slice. The times are simulated.
512 devices in a mesh: row: 32 (over y, x), col: 16 (over z, core).
Axes of the slice: x: 4, y: 8, z: 8, core: 2. Of those that a mesh axis runs over, the one named last changes fastest.
Arguments:
- activations: bfloat16 [384, 8192], P('row', 'col'), may hold values from -6 to 6
- gate_weight: bfloat16 [8192, 16384], P('col', 'row'), may hold values from -0.0625 to 0.0625
- up_weight: bfloat16 [8192, 16384], P('col', 'row'), may hold values from -0.0625 to 0.0625
- down_weight: bfloat16 [16384, 8192], P('row', 'col'), may hold values from -0.046875 to 0.046875
- out_grad: bfloat16 [384, 8192], P('row', 'col'), may hold values from -1.75 to 1.75
Outputs:
- layer_out: bfloat16 [384, 8192], P('row', 'col')
- input_grad: bfloat16 [384, 8192], P('row', 'col')
- gate_grad: float32 [8192, 16384], P('col', 'row')
- up_grad: float32 [8192, 16384], P('col', 'row')
- down_grad: float32 [16384, 8192], P('row', 'col')
All inputs are finite; a program needn't handle non-finite values.
Results may differ from a plain program's by a relative error of at most 0.005.
Values may be sent and summed in bfloat16 or wider, within the bound.
No kernel may reach another device: no remote copies, remote signals or barrier semaphores. Data moves between devices by JAX's collectives and lax.ppermute only.
A program may use at most 64 MiB of HBM per device.

v0:
```python
import jax
import jax.numpy as jnp
from jax import lax
from jax.sharding import PartitionSpec as P


def contract_rows(left_side, right_side):
    return lax.dot_general(
        left_side, right_side, (((0,), (0,)), ((), ())), preferred_element_type=jnp.float32
    )


def contract_cols(left_side, right_side):
    return lax.dot_general(
        left_side, right_side, (((1,), (1,)), ((), ())), preferred_element_type=jnp.float32
    )


def swiglu_deltas(hidden_grad, gate, up):
    gate_sigmoid = jax.nn.sigmoid(gate)
    gate_silu = gate * gate_sigmoid
    gate_delta = (hidden_grad * up * gate_sigmoid * (1.0 + gate * (1.0 - gate_sigmoid))).astype(
        jnp.bfloat16
    )
    up_delta = (hidden_grad * gate_silu).astype(jnp.bfloat16)
    return (gate_delta, up_delta)


def local(activations, gate_weight, up_weight, down_weight, out_grad):
    hidden_width = gate_weight.shape[1]
    feature_width = activations.shape[1]
    all_tokens, all_grads = (
        lax.all_gather(activations, "row", axis=0, tiled=True),
        lax.all_gather(out_grad, "row", axis=0, tiled=True),
    )
    both_weights = jnp.concatenate([gate_weight, up_weight], axis=1)
    picked = all_tokens
    summed = lax.psum_scatter(
        jnp.dot(picked, both_weights, preferred_element_type=jnp.float32),
        "col",
        scatter_dimension=0,
        tiled=True,
    )
    gate = summed[:, :hidden_width]
    up = summed[:, hidden_width:]
    hidden = (jax.nn.silu(gate) * up).astype(jnp.bfloat16)
    hidden_all = lax.all_gather(hidden, "col", axis=0, tiled=True)
    picked = all_grads
    hidden_grad = lax.psum_scatter(
        contract_cols(picked, down_weight), "col", scatter_dimension=0, tiled=True
    )
    gate_delta, up_delta = swiglu_deltas(hidden_grad, gate, up)
    all_gate_delta, all_up_delta = (
        lax.all_gather(gate_delta, "col", axis=0, tiled=True),
        lax.all_gather(up_delta, "col", axis=0, tiled=True),
    )
    gate_grad = contract_rows(all_tokens, all_gate_delta)
    up_grad = contract_rows(all_tokens, all_up_delta)
    down_grad = contract_rows(hidden_all, all_grads)
    forward_term = jnp.dot(hidden_all, down_weight, preferred_element_type=jnp.float32)
    backward_term = contract_cols(all_gate_delta, gate_weight) + contract_cols(
        all_up_delta, up_weight
    )
    row_total = lax.psum_scatter(
        jnp.concatenate([forward_term, backward_term], axis=1),
        "row",
        scatter_dimension=0,
        tiled=True,
    )
    layer_out = row_total[:, :feature_width].astype(jnp.bfloat16)
    input_grad = row_total[:, feature_width:].astype(jnp.bfloat16)
    return (layer_out, input_grad, gate_grad, up_grad, down_grad)


def solution(mesh):
    return jax.shard_map(
        local,
        mesh=mesh,
        in_specs=(
            P("row", "col"),
            P("col", "row"),
            P("col", "row"),
            P("row", "col"),
            P("row", "col"),
        ),
        out_specs=(
            P("row", "col"),
            P("row", "col"),
            P("col", "row"),
            P("col", "row"),
            P("row", "col"),
        ),
        check_vma=False,
    )
```

profile of v0, /device:TPU:64, one launch (start us, length us, event | category | flops | bytes accessed | tf_op | source)
XLA Modules:
  0.0 370.0 jit_solution(8546678322941645992)
XLA Ops:
  7.2 50.6 %all-gather.1 = bf16[32,12,512]{2,1,0:T(8,128)(2,1)S(1)} all-gather(bf16[1,12,512]{2,1,0:T(8,128)(2,1)} %bitcast.28), channel_id=1, replica_groups=mesh['row'=32,'col'=16] {'row'}, dimensions={0}, use_global_device_ids=true | all-gather | bytes 405504 | tf_op jit(solution)/shard_map/all_gather | solution.py:34
  58.0 1.3 fusion.9
  59.3 48.1 %all-gather = bf16[32,12,512]{2,1,0:T(8,128)(2,1)S(1)} all-gather(bf16[1,12,512]{2,1,0:T(8,128)(2,1)S(1)} %bitcast.29), channel_id=1, replica_groups=mesh['row'=32,'col'=16] {'row'}, dimensions={0}, use_global_device_ids=true | all-gather | bytes 405504 | tf_op jit(solution)/shard_map/all_gather | solution.py:33
  107.6 1.8 convolution_bitcast_fusion
  109.4 1.6 copy.30
  111.1 1.3 dynamic-slice.4
  113.0 4.8 %reduce-scatter.11.cloned.1.call-done = f32[24,512]{1,0:T(8,128)} async-done(((f32[384,512]{1,0:T(8,128)}), f32[24,512]{1,0:T(8,128)}) %reduce-scatter.11.cloned.1.call-update) | async-done | bytes 49168 | tf_op jit(solution)/shard_map/reduce_scatter | solution.py:49
  117.9 62.4 %reduce-scatter.9.cloned.1.call-done = f32[24,1024]{1,0:T(8,128)} async-done(((f32[384,1024]{1,0:T(8,128)}), f32[24,1024]{1,0:T(8,128)}) %reduce-scatter.9.cloned.1.call-update) | async-done | bytes 98320 | tf_op jit(solution)/shard_map/reduce_scatter | solution.py:38
  181.1 18.8 %all_gather.18 = bf16[384,512]{1,0:T(8,128)(2,1)S(1)} all-gather(bf16[24,512]{1,0:T(8,128)(2,1)S(1)} %get-tuple-element.26), channel_id=1, replica_groups=mesh['row'=32,'col'=16] {'col'}, dimensions={0}, use_global_device_ids=true | all-gather | bytes 417792 | tf_op jit(solution)/shard_map/all_gather | solution.py:54
  200.3 15.4 %all_gather.19 = bf16[384,512]{1,0:T(8,128)(2,1)S(1)} all-gather(bf16[24,512]{1,0:T(8,128)(2,1)S(1)} %get-tuple-element.25), channel_id=1, replica_groups=mesh['row'=32,'col'=16] {'col'}, dimensions={0}, use_global_device_ids=true | all-gather | bytes 417792 | tf_op jit(solution)/shard_map/all_gather | solution.py:55
  215.8 17.1 %all_gather.16 = bf16[384,512]{1,0:T(8,128)(2,1)S(1)} all-gather(bf16[24,512]{1,0:T(8,128)(2,1)S(1)} %get-tuple-element.27), channel_id=1, replica_groups=mesh['row'=32,'col'=16] {'col'}, dimensions={0}, use_global_device_ids=true | all-gather | bytes 417792 | tf_op jit(solution)/shard_map/all_gather | solution.py:47
  234.2 88.3 %fusion = f32[16,1024]{1,0:T(8,128)S(1)} fusion(f32[384,1024]{1,0:T(8,128)S(1)} %pad_maximum_fusion), kind=kCustom, calls=%all-reduce-scatter | all-reduce-scatter fusion | flops 524289 | bytes 1640448
  322.4 1.3 collective-permute-start
  323.7 1.3 collective-permute-start.1
  325.0 1.9 collective-permute-start.2
  326.9 1.9 collective-permute-start.3
  329.3 10.8 %collective-permute-start.7 = (bf16[12,1024]{1,0:T(8,128)(2,1)S(1)}, bf16[12,1024]{1,0:T(8,128)(2,1)S(1)}, u32[]{:S(2)}, u32[]{:S(2)}) collective-permute-start(bf16[12,1024]{1,0:T(8,128)(2,1)S(1)} %slice.22), channel_id=1, source_target_pairs={{0,128},{16,144},{32,160},{48,176},{64,192},{80,208},{96,224},{112... | collective-permute-start | bytes 73736
  341.7 2.2 collective-permute-start.4
  343.9 6.0 %collective-permute-start.5 = (bf16[16,1024]{1,0:T(8,128)(2,1)S(1)}, bf16[16,1024]{1,0:T(8,128)(2,1)S(1)}, u32[]{:S(2)}, u32[]{:S(2)}) collective-permute-start(bf16[16,1024]{1,0:T(8,128)(2,1)S(1)} %convert.20), channel_id=1, source_target_pairs={{0,96},{16,112},{32,128},{48,144},{64,160},{80,176},{96,192},{112,... | collective-permute-start | bytes 98312
  350.0 5.8 %collective-permute-start.6 = (bf16[16,1024]{1,0:T(8,128)(2,1)S(1)}, bf16[16,1024]{1,0:T(8,128)(2,1)S(1)}, u32[]{:S(2)}, u32[]{:S(2)}) collective-permute-start(bf16[16,1024]{1,0:T(8,128)(2,1)S(1)} %convert.20), channel_id=1, source_target_pairs={{0,112},{16,128},{32,144},{48,160},{64,176},{80,192},{96,208},{112... | collective-permute-start | bytes 98312
  355.8 1.4 fusion.11
  357.2 1.3 copy.27
  358.6 1.3 copy.28
  359.9 2.6 concatenate.8
  (51 shorter events, 5.6 us)
Async XLA Ops:
  7.2 50.8 %copy-start = (bf16[512,512]{1,0:T(8,128)(2,1)S(1)}, bf16[512,512]{1,0:T(8,128)(2,1)}, u32[]{:S(2)}) copy-start(bf16[512,512]{1,0:T(8,128)(2,1)} %param.8) | copy-start | bytes 1572868
  7.2 110.7 %reduce-scatter.11.cloned.1.call-start = ((), (), s32[]{:S(2)}) async-start(), calls=%async_computation.3 | async-start | bytes 835584 | tf_op jit(solution)/shard_map/reduce_scatter | solution.py:49
  57.8 1.5 copy-start.12
  57.9 49.6 %copy-start.1 = (bf16[384,512]{1,0:T(8,128)(2,1)}, bf16[384,512]{1,0:T(8,128)(2,1)S(1)}, u32[]{:S(2)}) copy-start(bf16[384,512]{1,0:T(8,128)(2,1)S(1)} %reshape.13) | copy-start | bytes 1179652
  57.9 49.6 %copy-start.5 = (bf16[512,512]{1,0:T(8,128)(2,1)S(1)}, bf16[512,512]{1,0:T(8,128)(2,1)}, u32[]{:S(2)}) copy-start(bf16[512,512]{1,0:T(8,128)(2,1)} %param.7) | copy-start | bytes 1572868
  59.3 121.0 %reduce-scatter.9.cloned.1.call-start = ((), (), s32[]{:S(2)}) async-start(), calls=%async_computation.2 | async-start | bytes 1671168 | tf_op jit(solution)/shard_map/reduce_scatter | solution.py:38
  111.0 88.9 %copy-start.7 = (bf16[512,512]{1,0:T(8,128)(2,1)S(1)}, bf16[512,512]{1,0:T(8,128)(2,1)}, u32[]{:S(2)}) copy-start(bf16[512,512]{1,0:T(8,128)(2,1)} %param.6) | copy-start | bytes 1572868
  200.3 33.3 %copy-start.6 = (bf16[512,512]{1,0:T(8,128)(2,1)S(1)}, bf16[512,512]{1,0:T(8,128)(2,1)}, u32[]{:S(2)}) copy-start(bf16[512,512]{1,0:T(8,128)(2,1)} %param.7) | copy-start | bytes 1572868
  232.9 0.7 copy-start.3
  322.4 21.5 %collective-permute-start = (bf16[16,1024]{1,0:T(8,128)(2,1)S(1)}, bf16[16,1024]{1,0:T(8,128)(2,1)S(1)}, u32[]{:S(2)}, u32[]{:S(2)}) collective-permute-start(bf16[16,1024]{1,0:T(8,128)(2,1)S(1)} %convert.20), channel_id=1, source_target_pairs={{0,16},{16,32},{32,48},{48,64},{64,80},{80,96},{96,112},{112,128},... | collective-permute-start | bytes 98312
  323.7 26.2 %collective-permute-start.1 = (bf16[16,1024]{1,0:T(8,128)(2,1)S(1)}, bf16[16,1024]{1,0:T(8,128)(2,1)S(1)}, u32[]{:S(2)}, u32[]{:S(2)}) collective-permute-start(bf16[16,1024]{1,0:T(8,128)(2,1)S(1)} %convert.20), channel_id=1, source_target_pairs={{0,32},{16,48},{32,64},{48,80},{64,96},{80,112},{96,128},{112,144}... | collective-permute-start | bytes 98312
  325.0 34.8 %collective-permute-start.2 = (bf16[16,1024]{1,0:T(8,128)(2,1)S(1)}, bf16[16,1024]{1,0:T(8,128)(2,1)}, u32[]{:S(2)}, u32[]{:S(2)}) collective-permute-start(bf16[16,1024]{1,0:T(8,128)(2,1)S(1)} %convert.20), channel_id=1, source_target_pairs={{0,48},{16,64},{32,80},{48,96},{64,112},{80,128},{96,144},{112,160... | collective-permute-start | bytes 98312
  326.9 32.9 %collective-permute-start.3 = (bf16[16,1024]{1,0:T(8,128)(2,1)S(1)}, bf16[16,1024]{1,0:T(8,128)(2,1)}, u32[]{:S(2)}, u32[]{:S(2)}) collective-permute-start(bf16[16,1024]{1,0:T(8,128)(2,1)S(1)} %convert.20), channel_id=1, source_target_pairs={{0,64},{16,80},{32,96},{48,112},{64,128},{80,144},{96,160},{112,17... | collective-permute-start | bytes 98312
  328.8 27.0 %copy-start.2 = (bf16[384,512]{1,0:T(8,128)(2,1)S(1)}, bf16[384,512]{1,0:T(8,128)(2,1)}, u32[]{:S(2)}) copy-start(bf16[384,512]{1,0:T(8,128)(2,1)} %copy-done.1) | copy-start | bytes 1179652
  328.9 27.0 %copy-start.4 = (bf16[384,512]{1,0:T(8,128)(2,1)S(1)}, bf16[384,512]{1,0:T(8,128)(2,1)}, u32[]{:S(2)}) copy-start(bf16[384,512]{1,0:T(8,128)(2,1)} %copy-done.3) | copy-start | bytes 1179652
  329.3 12.4 %collective-permute-start.7 = (bf16[12,1024]{1,0:T(8,128)(2,1)S(1)}, bf16[12,1024]{1,0:T(8,128)(2,1)S(1)}, u32[]{:S(2)}, u32[]{:S(2)}) collective-permute-start(bf16[12,1024]{1,0:T(8,128)(2,1)S(1)} %slice.22), channel_id=1, source_target_pairs={{0,128},{16,144},{32,160},{48,176},{64,192},{80,208},{96,224},{112... | collective-permute-start | bytes 73736
  341.7 14.1 %copy-start.10 = (bf16[12,1024]{1,0:T(8,128)(2,1)}, bf16[12,1024]{1,0:T(8,128)(2,1)S(1)}, u32[]{:S(2)}) copy-start(bf16[12,1024]{1,0:T(8,128)(2,1)S(1)} %collective-permute-done.7) | copy-start | bytes 73732
  341.7 18.2 %collective-permute-start.4 = (bf16[16,1024]{1,0:T(8,128)(2,1)S(1)}, bf16[16,1024]{1,0:T(8,128)(2,1)S(1)}, u32[]{:S(2)}, u32[]{:S(2)}) collective-permute-start(bf16[16,1024]{1,0:T(8,128)(2,1)S(1)} %convert.20), channel_id=1, source_target_pairs={{0,80},{16,96},{32,112},{48,128},{64,144},{80,160},{96,176},{112,1... | collective-permute-start | bytes 98312
  343.9 15.9 %collective-permute-start.5 = (bf16[16,1024]{1,0:T(8,128)(2,1)S(1)}, bf16[16,1024]{1,0:T(8,128)(2,1)S(1)}, u32[]{:S(2)}, u32[]{:S(2)}) collective-permute-start(bf16[16,1024]{1,0:T(8,128)(2,1)S(1)} %convert.20), channel_id=1, source_target_pairs={{0,96},{16,112},{32,128},{48,144},{64,160},{80,176},{96,192},{112,... | collective-permute-start | bytes 98312
  350.0 5.8 %copy-start.8 = (bf16[16,1024]{1,0:T(8,128)(2,1)}, bf16[16,1024]{1,0:T(8,128)(2,1)S(1)}, u32[]{:S(2)}) copy-start(bf16[16,1024]{1,0:T(8,128)(2,1)S(1)} %collective-permute-done.1) | copy-start | bytes 98308
  350.0 9.9 %collective-permute-start.6 = (bf16[16,1024]{1,0:T(8,128)(2,1)S(1)}, bf16[16,1024]{1,0:T(8,128)(2,1)S(1)}, u32[]{:S(2)}, u32[]{:S(2)}) collective-permute-start(bf16[16,1024]{1,0:T(8,128)(2,1)S(1)} %convert.20), channel_id=1, source_target_pairs={{0,112},{16,128},{32,144},{48,160},{64,176},{80,192},{96,208},{112... | collective-permute-start | bytes 98312
  358.6 1.3 copy-start.9
  358.6 1.4 copy-start.11
Sparse Core Ops, SparseCore 0:
  59.4 58.4 reduce-scatter.10
  120.9 59.2 reduce-scatter.8
where the time goes:
time: 371 us; the launch traced here: 370 us
  blocking collectives  238 us (64%)
  waiting for transfers between devices  68.4 us (18%)
  starting transfers between devices  31.3 us (8%)
  between operations  15 us (4%)
  local copies, waits for them, and re-layouts  9.43 us (3%)
  matrix products  6.56 us (2%)
    unnamed x1, blocking collectives  88.3 us
    reduce_scatter x1, waiting for transfers between devices, local(): lax.psum_scatter(jnp.dot(picked, both_weights, preferred_element_type=jnp...  62.4 us
    all_gather x1, blocking collectives, local(): lax.all_gather(out_grad, 'row', axis=0, tiled=True)  50.6 us
    all_gather x1, blocking collectives, local(): lax.all_gather(activations, 'row', axis=0, tiled=True)  48.1 us
    unnamed x8, starting transfers between devices  31.2 us
    all_gather x1, blocking collectives, local(): lax.all_gather(gate_delta, 'col', axis=0, tiled=True)  18.8 us
    all_gather x1, blocking collectives, local(): hidden_all = lax.all_gather(hidden, 'col', axis=0, tiled=True)  17.1 us
    all_gather x1, blocking collectives, local(): lax.all_gather(up_delta, 'col', axis=0, tiled=True)  15.4 us
  transfers between devices with their start and end apart: 10, of which 3 were waited for; matrix products, arithmetic and copies ran while one was open for 3% of the time, Pallas kernels for 0%

commit v1 on v0

--- a/solution.py
+++ b/solution.py
@@ -51,7 +51,9 @@
     )
     gate_delta, up_delta = swiglu_deltas(hidden_grad, gate, up)
     all_gate_delta, all_up_delta = (
-        lax.all_gather(gate_delta, "col", axis=0, tiled=True),
+        jnp.concatenate(
+            lax.all_to_all(jnp.stack([gate_delta] * lax.axis_size("col")), "col", 0, 0), axis=0
+        ),
         lax.all_gather(up_delta, "col", axis=0, tiled=True),
     )
     gate_grad = contract_rows(all_tokens, all_gate_delta)

time: 371 us -> 367 us (0.989)
  the two profiles are of different devices: /device:TPU:64 before, /device:TPU:14 now
where the time goes in v1:
time: 367 us; the launch traced here: 366 us
  blocking collectives  215 us (59%)
  waiting for transfers between devices  75.4 us (21%)
  starting transfers between devices  38.5 us (10%)
  between operations  15 us (4%)
  local copies, waits for them, and re-layouts  10.6 us (3%)
  matrix products  9.75 us (3%)
    unnamed x1, blocking collectives  76.1 us
    reduce_scatter x1, waiting for transfers between devices, local(): lax.psum_scatter(jnp.dot(picked, both_weights, preferred_element_type=jnp...  62.6 us
    all_gather x1, blocking collectives, local(): lax.all_gather(out_grad, 'row', axis=0, tiled=True)  50.1 us
    all_gather x1, blocking collectives, local(): lax.all_gather(activations, 'row', axis=0, tiled=True)  48.8 us
    unnamed x8, starting transfers between devices  34.6 us
    all_gather x1, blocking collectives, local(): lax.all_gather(up_delta, 'col', axis=0, tiled=True)  24.2 us
    all_gather x1, blocking collectives, local(): hidden_all = lax.all_gather(hidden, 'col', axis=0, tiled=True)  15.5 us
    unnamed x26, local copies, waits for them, and re-layouts  9.22 us
  transfers between devices with their start and end apart: 11, of which 4 were waited for; matrix products, arithmetic and copies ran while one was open for 4% of the time, Pallas kernels for 0%

profile of v1, /device:TPU:14, one launch (start us, length us, event | category | flops | bytes accessed | tf_op | source)
XLA Modules:
  0.0 365.7 jit_solution(18142501370121096713)
XLA Ops:
  7.2 50.1 %all-gather.1 = bf16[32,12,512]{2,1,0:T(8,128)(2,1)S(1)} all-gather(bf16[1,12,512]{2,1,0:T(8,128)(2,1)} %bitcast.31), channel_id=1, replica_groups=mesh['row'=32,'col'=16] {'row'}, dimensions={0}, use_global_device_ids=true | all-gather | bytes 405504 | tf_op jit(solution)/shard_map/all_gather | solution.py:34
  58.8 48.8 %all-gather = bf16[32,12,512]{2,1,0:T(8,128)(2,1)S(1)} all-gather(bf16[1,12,512]{2,1,0:T(8,128)(2,1)S(1)} %bitcast.32), channel_id=1, replica_groups=mesh['row'=32,'col'=16] {'row'}, dimensions={0}, use_global_device_ids=true | all-gather | bytes 405504 | tf_op jit(solution)/shard_map/all_gather | solution.py:33
  107.7 1.8 convolution_bitcast_fusion
  109.5 1.6 copy.32
  113.1 8.6 %reduce-scatter.11.cloned.1.call-done = f32[24,512]{1,0:T(8,128)} async-done(((f32[384,512]{1,0:T(8,128)}), f32[24,512]{1,0:T(8,128)}) %reduce-scatter.11.cloned.1.call-update) | async-done | bytes 49168 | tf_op jit(solution)/shard_map/reduce_scatter | solution.py:49
  121.6 62.6 %reduce-scatter.9.cloned.1.call-done = f32[24,1024]{1,0:T(8,128)} async-done(((f32[384,1024]{1,0:T(8,128)}), f32[24,1024]{1,0:T(8,128)}) %reduce-scatter.9.cloned.1.call-update) | async-done | bytes 98320 | tf_op jit(solution)/shard_map/reduce_scatter | solution.py:38
  185.9 3.8 %all-to-all-start = ((bf16[16,24,512]{2,1,0:T(8,128)(2,1)}), bf16[16,24,512]{2,1,0:T(8,128)(2,1)S(1)}, u32[]{:S(2)}, u32[]{:S(2)}) async-start(bf16[16,24,512]{2,1,0:T(8,128)(2,1)} %stack.2), calls=%async_computation | async-start | bytes 786432 | tf_op jit(solution)/shard_map/all_to_all | solution.py:55
  189.7 24.2 %all_gather.15 = bf16[384,512]{1,0:T(8,128)(2,1)S(1)} all-gather(bf16[24,512]{1,0:T(8,128)(2,1)S(1)} %get-tuple-element.25), channel_id=1, replica_groups=mesh['row'=32,'col'=16] {'col'}, dimensions={0}, use_global_device_ids=true | all-gather | bytes 417792 | tf_op jit(solution)/shard_map/all_gather | solution.py:57
  213.9 15.5 %all_gather.13 = bf16[384,512]{1,0:T(8,128)(2,1)S(1)} all-gather(bf16[24,512]{1,0:T(8,128)(2,1)S(1)} %get-tuple-element.27), channel_id=1, replica_groups=mesh['row'=32,'col'=16] {'col'}, dimensions={0}, use_global_device_ids=true | all-gather | bytes 417792 | tf_op jit(solution)/shard_map/all_gather | solution.py:47
  231.9 1.6 fusion.10
  234.7 76.1 %fusion = f32[16,1024]{1,0:T(8,128)} fusion(f32[384,1024]{1,0:T(8,128)S(1)} %pad_maximum_fusion), kind=kCustom, calls=%all-reduce-scatter | all-reduce-scatter fusion | flops 524289 | bytes 1640448
  311.6 4.2 %collective-permute-start = (bf16[16,1024]{1,0:T(8,128)(2,1)S(1)}, bf16[16,1024]{1,0:T(8,128)(2,1)S(1)}, u32[]{:S(2)}, u32[]{:S(2)}) collective-permute-start(bf16[16,1024]{1,0:T(8,128)(2,1)S(1)} %convert.20), channel_id=1, source_target_pairs={{0,16},{16,32},{32,48},{48,64},{64,80},{80,96},{96,112},{112,128},... | collective-permute-start | bytes 98312
  315.8 5.8 %collective-permute-start.1 = (bf16[16,1024]{1,0:T(8,128)(2,1)S(1)}, bf16[16,1024]{1,0:T(8,128)(2,1)S(1)}, u32[]{:S(2)}, u32[]{:S(2)}) collective-permute-start(bf16[16,1024]{1,0:T(8,128)(2,1)S(1)} %convert.20), channel_id=1, source_target_pairs={{0,32},{16,48},{32,64},{48,80},{64,96},{80,112},{96,128},{112,144}... | collective-permute-start | bytes 98312
  322.5 12.0 %collective-permute-start.7 = (bf16[12,1024]{1,0:T(8,128)(2,1)S(1)}, bf16[12,1024]{1,0:T(8,128)(2,1)S(1)}, u32[]{:S(2)}, u32[]{:S(2)}) collective-permute-start(bf16[12,1024]{1,0:T(8,128)(2,1)S(1)} %slice.22), channel_id=1, source_target_pairs={{0,128},{16,144},{32,160},{48,176},{64,192},{80,208},{96,224},{112... | collective-permute-start | bytes 73736
  334.4 2.5 fusion.11
  337.0 1.3 copy.30
  338.3 2.0 collective-permute-start.2
  340.3 2.8 collective-permute-start.3
  343.2 3.7 %collective-permute-start.4 = (bf16[16,1024]{1,0:T(8,128)(2,1)S(1)}, bf16[16,1024]{1,0:T(8,128)(2,1)S(1)}, u32[]{:S(2)}, u32[]{:S(2)}) collective-permute-start(bf16[16,1024]{1,0:T(8,128)(2,1)S(1)} %convert.20), channel_id=1, source_target_pairs={{0,80},{16,96},{32,112},{48,128},{64,144},{80,160},{96,176},{112,1... | collective-permute-start | bytes 98312
  346.9 2.2 collective-permute-start.5
  349.1 1.9 collective-permute-start.6
  351.5 1.3 copy.29
  352.8 2.3 collective-permute-done.5
  355.1 1.9 collective-permute-done.6
  (45 shorter events, 12.2 us)
Async XLA Ops:
  7.2 50.3 %copy-start = (bf16[512,512]{1,0:T(8,128)(2,1)S(1)}, bf16[512,512]{1,0:T(8,128)(2,1)}, u32[]{:S(2)}) copy-start(bf16[512,512]{1,0:T(8,128)(2,1)} %param.8) | copy-start | bytes 1572868
  7.2 114.5 %reduce-scatter.11.cloned.1.call-start = ((), (), s32[]{:S(2)}) async-start(), calls=%async_computation.4 | async-start | bytes 835584 | tf_op jit(solution)/shard_map/reduce_scatter | solution.py:49
  57.3 1.5 copy-start.8
  57.4 1.4 copy-start.1
  57.4 50.2 %copy-start.7 = (bf16[512,512]{1,0:T(8,128)(2,1)S(1)}, bf16[512,512]{1,0:T(8,128)(2,1)}, u32[]{:S(2)}) copy-start(bf16[512,512]{1,0:T(8,128)(2,1)} %param.7) | copy-start | bytes 1572868
  58.8 125.5 %reduce-scatter.9.cloned.1.call-start = ((), (), s32[]{:S(2)}) async-start(), calls=%async_computation.3 | async-start | bytes 1671168 | tf_op jit(solution)/shard_map/reduce_scatter | solution.py:38
  185.9 46.0 %all-to-all-start = ((bf16[16,24,512]{2,1,0:T(8,128)(2,1)}), bf16[16,24,512]{2,1,0:T(8,128)(2,1)S(1)}, u32[]{:S(2)}, u32[]{:S(2)}) async-start(bf16[16,24,512]{2,1,0:T(8,128)(2,1)} %stack.2), calls=%async_computation | async-start | bytes 786432 | tf_op jit(solution)/shard_map/all_to_all | solution.py:55
  229.4 0.8 copy-start.4
  231.8 1.6 copy-start.2
  233.4 1.1 copy-start.5
  311.6 35.2 %collective-permute-start = (bf16[16,1024]{1,0:T(8,128)(2,1)S(1)}, bf16[16,1024]{1,0:T(8,128)(2,1)S(1)}, u32[]{:S(2)}, u32[]{:S(2)}) collective-permute-start(bf16[16,1024]{1,0:T(8,128)(2,1)S(1)} %convert.20), channel_id=1, source_target_pairs={{0,16},{16,32},{32,48},{48,64},{64,80},{80,96},{96,112},{112,128},... | collective-permute-start | bytes 98312
  315.8 33.3 %collective-permute-start.1 = (bf16[16,1024]{1,0:T(8,128)(2,1)S(1)}, bf16[16,1024]{1,0:T(8,128)(2,1)S(1)}, u32[]{:S(2)}, u32[]{:S(2)}) collective-permute-start(bf16[16,1024]{1,0:T(8,128)(2,1)S(1)} %convert.20), channel_id=1, source_target_pairs={{0,32},{16,48},{32,64},{48,80},{64,96},{80,112},{96,128},{112,144}... | collective-permute-start | bytes 98312
  322.5 28.6 %copy-start.3 = (bf16[16,24,512]{2,1,0:T(8,128)(2,1)S(1)}, bf16[16,24,512]{2,1,0:T(8,128)(2,1)}, u32[]{:S(2)}) copy-start(bf16[16,24,512]{2,1,0:T(8,128)(2,1)} %copy-done.2) | copy-start | bytes 1179652
  322.5 20.7 %collective-permute-start.7 = (bf16[12,1024]{1,0:T(8,128)(2,1)S(1)}, bf16[12,1024]{1,0:T(8,128)(2,1)S(1)}, u32[]{:S(2)}, u32[]{:S(2)}) collective-permute-start(bf16[12,1024]{1,0:T(8,128)(2,1)S(1)} %slice.22), channel_id=1, source_target_pairs={{0,128},{16,144},{32,160},{48,176},{64,192},{80,208},{96,224},{112... | collective-permute-start | bytes 73736
  338.3 18.7 %copy-start.6 = (f32[16,1024]{1,0:T(8,128)S(1)}, f32[16,1024]{1,0:T(8,128)}, u32[]{:S(2)}) copy-start(f32[16,1024]{1,0:T(8,128)} %fusion) | copy-start | bytes 196612
  338.3 14.5 %collective-permute-start.2 = (bf16[16,1024]{1,0:T(8,128)(2,1)S(1)}, bf16[16,1024]{1,0:T(8,128)(2,1)S(1)}, u32[]{:S(2)}, u32[]{:S(2)}) collective-permute-start(bf16[16,1024]{1,0:T(8,128)(2,1)S(1)} %convert.20), channel_id=1, source_target_pairs={{0,48},{16,64},{32,80},{48,96},{64,112},{80,128},{96,144},{112,160... | collective-permute-start | bytes 98312
  340.3 12.5 %collective-permute-start.3 = (bf16[16,1024]{1,0:T(8,128)(2,1)S(1)}, bf16[16,1024]{1,0:T(8,128)(2,1)S(1)}, u32[]{:S(2)}, u32[]{:S(2)}) collective-permute-start(bf16[16,1024]{1,0:T(8,128)(2,1)S(1)} %convert.20), channel_id=1, source_target_pairs={{0,64},{16,80},{32,96},{48,112},{64,128},{80,144},{96,160},{112,17... | collective-permute-start | bytes 98312
  343.2 9.7 %collective-permute-start.4 = (bf16[16,1024]{1,0:T(8,128)(2,1)S(1)}, bf16[16,1024]{1,0:T(8,128)(2,1)S(1)}, u32[]{:S(2)}, u32[]{:S(2)}) collective-permute-start(bf16[16,1024]{1,0:T(8,128)(2,1)S(1)} %convert.20), channel_id=1, source_target_pairs={{0,80},{16,96},{32,112},{48,128},{64,144},{80,160},{96,176},{112,1... | collective-permute-start | bytes 98312
  346.9 8.2 %collective-permute-start.5 = (bf16[16,1024]{1,0:T(8,128)(2,1)S(1)}, bf16[16,1024]{1,0:T(8,128)(2,1)S(1)}, u32[]{:S(2)}, u32[]{:S(2)}) collective-permute-start(bf16[16,1024]{1,0:T(8,128)(2,1)S(1)} %convert.20), channel_id=1, source_target_pairs={{0,96},{16,112},{32,128},{48,144},{64,160},{80,176},{96,192},{112,... | collective-permute-start | bytes 98312
  349.1 7.9 %collective-permute-start.6 = (bf16[16,1024]{1,0:T(8,128)(2,1)S(1)}, bf16[16,1024]{1,0:T(8,128)(2,1)S(1)}, u32[]{:S(2)}, u32[]{:S(2)}) collective-permute-start(bf16[16,1024]{1,0:T(8,128)(2,1)S(1)} %convert.20), channel_id=1, source_target_pairs={{0,112},{16,128},{32,144},{48,160},{64,176},{80,192},{96,208},{112... | collective-permute-start | bytes 98312
Sparse Core Ops, SparseCore 0:
  58.9 62.7 reduce-scatter.10
  124.7 59.4 reduce-scatter.8
